TPU v7x, 32 devices: a whole 2x2x4 slice. The times are simulated.
32 devices in a mesh: grp: 2 (over x), tp: 8 (over z, y), rb: 2 (over core).
Axes of the slice: x: 2, y: 2, z: 4, core: 2. Of those that a mesh axis runs over, the one named last changes fastest.
Arguments:
- peram: bfloat16 [2048, 24, 2, 1024], P(('grp', 'tp'), None, None, 'rb'), parts along dimension 0, may hold values from -1 to 1
- src_elems: bfloat16 [14, 2, 256, 256], P('grp'), parts along dimension 0, may hold values from -0.25 to 0.25
- owner_times: int32 [16, 2], P('grp'), parts along dimension 0, may hold values from 0 to 23
- diag_mom: int32 [16, 2, 2], P(('grp', 'tp')), parts along dimension 0, may hold values from 0 to 6
- diag_count: int32 [16], P(('grp', 'tp')), parts along dimension 0, may hold values from 1 to 2, as said below
Outputs:
- corr: float32 [16, 2, 2, 2], P(('grp', 'tp')), parts along dimension 0
There are 2 independent parts, one for each index of `grp`. A program takes and returns all parts, laid end to end along the dimension named above; each array names one. Nothing has to cross between parts.
Inputs may be any that keep to these rules, and one draw needn't show every extreme that they name: `diag_count`: some pair has 2 assignments.
All inputs are finite; a program needn't handle non-finite values.
Results may differ from a plain program's by a relative error of at most 0.0031.
Values may be sent and summed in bfloat16 or wider, within the bound.
A program may use at most 128 MiB of HBM per device.

v0:
```python
import jax
import jax.numpy as jnp
from jax import lax
from jax.sharding import PartitionSpec as P


def paired_rhs(factor_part):
    swapped = jnp.stack([factor_part[:, 1], -factor_part[:, 0]], axis=1)
    return jnp.stack([factor_part, swapped], axis=0)


def contract_rows(left_rows, right_pair):
    return lax.dot_general(
        left_rows, right_pair, (((1, 2), (2, 3)), ((), ())), preferred_element_type=jnp.float32
    )


def trace_block(flipped, diag_block):
    block_f = diag_block.astype(jnp.float32)
    flip_f = flipped.astype(jnp.float32)
    real_sum = jnp.sum(flip_f[0] * block_f[:, 0] - flip_f[1] * block_f[:, 1])
    imag_sum = jnp.sum(flip_f[0] * block_f[:, 1] + flip_f[1] * block_f[:, 0])
    return (real_sum, imag_sum)


def shards(peram, src_elems, owner_times, diag_mom, diag_count):
    rb_count = lax.axis_size("rb")
    rb_rank = lax.axis_index("rb")
    picked = jnp.take(peram, owner_times, axis=1)
    arrived = lax.all_to_all(picked, "tp", split_axis=1, concat_axis=0, tiled=True)
    factor = arrived[:, 0]
    total_rows = factor.shape[0]
    row_count = total_rows // rb_count
    eig_count = src_elems.shape[-1]
    spin_total = total_rows // eig_count
    local_spins = row_count // eig_count
    diag_total = diag_mom.shape[1]
    right_pairs = [paired_rhs(factor[:, time_slot]) for time_slot in range(2)]
    summed = lax.psum_scatter(
        jnp.stack(
            [contract_rows(factor[:, time_slot], right_pairs[time_slot]) for time_slot in range(2)],
            axis=1,
        ),
        "rb",
        scatter_dimension=0,
        tiled=True,
    )
    meson_rows = summed.astype(jnp.bfloat16)
    meson_a = meson_rows[:, 0]
    meson_b = meson_rows[:, 1]
    owned = diag_count[0]
    results = []
    for slot_index in range(diag_total):
        elem_three = lax.dynamic_index_in_dim(
            src_elems, diag_mom[0, slot_index, 0], 0, keepdims=False
        )
        elem_four = lax.dynamic_index_in_dim(
            src_elems, diag_mom[0, slot_index, 1], 0, keepdims=False
        )
        flip_three = jnp.swapaxes(elem_three, 1, 2)
        flip_four = jnp.swapaxes(elem_four, 1, 2)
        right_four = jnp.stack(
            [
                jnp.stack([elem_four[0], elem_four[1]], axis=1),
                jnp.stack([-elem_four[1], elem_four[0]], axis=1),
            ],
            axis=0,
        )
        left_three = jnp.stack(
            [
                jnp.stack([flip_three[0], flip_three[1]], axis=-1),
                jnp.stack([flip_three[1], -flip_three[0]], axis=-1),
            ],
            axis=1,
        )
        mixed = jnp.concatenate(
            [
                lax.dot_general(
                    left_three,
                    meson_a[spin_local * eig_count : (spin_local + 1) * eig_count],
                    (((2, 3), (0, 1)), ((), ())),
                    preferred_element_type=jnp.float32,
                )
                for spin_local in range(local_spins)
            ],
            axis=0,
        )
        cross_re = jnp.zeros((), jnp.float32)
        cross_im = jnp.zeros((), jnp.float32)
        for spin_index in range(spin_total):
            col_block = meson_b[:, :, spin_index * eig_count : (spin_index + 1) * eig_count]
            product = lax.dot_general(
                col_block,
                right_four,
                (((1, 2), (0, 1)), ((), ())),
                preferred_element_type=jnp.float32,
            )
            partner = mixed[:, :, spin_index * eig_count : (spin_index + 1) * eig_count]
            cross_re = cross_re + jnp.sum(
                product[:, 0] * partner[:, 0] - product[:, 1] * partner[:, 1]
            )
            cross_im = cross_im + jnp.sum(
                product[:, 0] * partner[:, 1] + product[:, 1] * partner[:, 0]
            )
        three_re = jnp.zeros((), jnp.float32)
        three_im = jnp.zeros((), jnp.float32)
        four_re = jnp.zeros((), jnp.float32)
        four_im = jnp.zeros((), jnp.float32)
        for spin_local in range(local_spins):
            global_spin = rb_rank * local_spins + spin_local
            block_a = lax.dynamic_slice_in_dim(
                meson_a[spin_local * eig_count : (spin_local + 1) * eig_count],
                global_spin * eig_count,
                eig_count,
                2,
            )
            block_b = lax.dynamic_slice_in_dim(
                meson_b[spin_local * eig_count : (spin_local + 1) * eig_count],
                global_spin * eig_count,
                eig_count,
                2,
            )
            add_re, add_im = trace_block(flip_three, block_a)
            three_re = three_re + add_re
            three_im = three_im + add_im
            add_re, add_im = trace_block(flip_four, block_b)
            four_re = four_re + add_re
            four_im = four_im + add_im
        values = jnp.stack([cross_re, cross_im, three_re, three_im, four_re, four_im])
        values = lax.psum(values, "rb")
        results.append(values)
    stacked = jnp.stack(results)
    direct_re = stacked[:, 2] * stacked[:, 4] - stacked[:, 3] * stacked[:, 5]
    direct_im = stacked[:, 2] * stacked[:, 5] + stacked[:, 3] * stacked[:, 4]
    direct = jnp.stack([direct_re, direct_im], axis=-1)
    crossed = stacked[:, 0:2]
    values_all = 0.25 * jnp.stack([direct, crossed], axis=1)
    keep = (jnp.arange(diag_total, dtype=jnp.int32) < owned)[:, None, None]
    return jnp.where(keep, values_all, jnp.zeros_like(values_all))[None]


def solution(mesh):
    in_specs = (
        P(("grp", "tp"), None, None, "rb"),
        P("grp", None, None, None),
        P("grp", None),
        P(("grp", "tp"), None, None),
        P(("grp", "tp")),
    )
    out_specs = P(("grp", "tp"), None, None, None)
    return jax.shard_map(shards, mesh=mesh, in_specs=in_specs, out_specs=out_specs, check_vma=False)
```

profile of v0, /device:TPU:9, one launch (start us, length us, event | category | flops | bytes accessed | tf_op | source)
XLA Modules:
  0.0 232.9 jit_solution(16534536423233338884)
XLA Ops:
  8.1 13.5 %gather_fusion = bf16[16,128,2,512]{3,2,1,0:T(2,128)(2,1)} fusion(bf16[128,24,2,512]{3,2,1,0:T(2,128)(2,1)} %param.5, s32[1024]{0:T(1024)S(1)} %pad_clamp_fusion), kind=kCustom, calls=%fused_computation | custom fusion | bytes 8388672 | tf_op jit(solution)/shard_map/jit(_take)/gather | solution.py:29
  21.6 5.1 %copy.38 = bf16[16,128,2,512]{3,1,2,0:T(8,128)(2,1)} copy(bf16[16,128,2,512]{3,2,1,0:T(2,128)(2,1)} %gather_fusion) | data formatting | bytes 8388608 | tf_op jit(solution)/shard_map/jit(_take)/gather | solution.py:29
  26.8 2.6 %select_bitcast_fusion = bf16[128,8,2,2,512]{4,0,3,2,1:T(8,128)(2,1)S(1)} fusion(bf16[8,2,128,2,512]{4,2,3,1,0:T(8,128)(2,1)} %bitcast.384, pred[8,2]{1,0:T(8,128)(4,1)S(1)} %copy.36), kind=kLoop, calls=%fused_computation.38 | loop fusion | flops 2097152 | bytes 8388624 | tf_op jit(solution)/shard_map/jit(_take)/select_n | solution.py:29
  29.5 96.9 %all_to_all.15 = bf16[128,8,2,2,512]{4,0,3,2,1:T(8,128)(2,1)S(1)} all-to-all(bf16[128,8,2,2,512]{4,0,3,2,1:T(8,128)(2,1)S(1)} %select_bitcast_fusion), channel_id=1, replica_groups=mesh['grp'=2,'tp'=8,'rb'=2] {'tp'}, dimensions={1} | all-to-all | bytes 8388608 | tf_op jit(solution)/shard_map/all_to_all | solution.py:30
  128.0 4.5 %fusion.8 = f32[1024,1,2,1024]{3,0,2,1:T(8,128)S(1)} fusion(bf16[1,1024,2,512]{3,1,2,0:T(8,128)(2,1)S(1)} %maximum_bitcast_fusion.1, bf16[1,1024,2,512]{3,1,2,0:T(8,128)(2,1)S(1)} %get-tuple-element.62, bf16[1024,2,2,512]{3,0,2,1:T(8,128)(2,1)S(1)} %bitcast.382), kind=kOutput, calls=%fused_computation.39 | convolution fusion | flops 4303355904 | bytes 14680064 | tf_op jit(solution)/shard_map/dot_general | solution.py:13
  132.7 4.5 %fusion.11 = f32[1024,1,2,1024]{3,0,2,1:T(8,128)S(1)} fusion(bf16[1,1024,2,512]{3,1,2,0:T(8,128)(2,1)S(1)} %maximum_bitcast_fusion, bf16[1,1024,2,512]{3,1,2,0:T(8,128)(2,1)S(1)} %get-tuple-element.61, bf16[1024,2,2,512]{3,0,2,1:T(8,128)(2,1)S(1)} %bitcast.383), kind=kOutput, calls=%fused_computation.40 | convolution fusion | flops 4303355904 | bytes 14680064 | tf_op jit(solution)/shard_map/dot_general | solution.py:13
  137.3 6.6 %pad_maximum_fusion = f32[1024,2,2,1024]{3,0,2,1:T(8,128)} fusion(f32[1024,1,2,1024]{3,0,2,1:T(8,128)S(1)} %fusion.8, f32[1024,1,2,1024]{3,0,2,1:T(8,128)S(1)} %fusion.11), kind=kLoop, calls=%fused_computation.1 | loop fusion | flops 4194304 | bytes 33554432 | tf_op jit(solution)/shard_map/stack | solution.py:40
  155.8 1.1 bitcast_convert_fusion.4
  156.9 0.9 convert_bitcast_fusion
  157.8 12.9 %reduce-scatter.2.cloned.1.call-done = f32[512,2,2,1024]{3,0,2,1:T(8,128)} async-done(((f32[1024,2,2,1024]{3,0,2,1:T(8,128)}), f32[512,2,2,1024]{3,0,2,1:T(8,128)}) %reduce-scatter.2.cloned.1.call-update) | async-done | bytes 8388624 | tf_op jit(solution)/shard_map/reduce_scatter | solution.py:39
  170.7 4.0 %convert_element_type.59 = bf16[512,2,2,1024]{3,0,2,1:T(8,128)(2,1)S(1)} convert(f32[512,2,2,1024]{3,0,2,1:T(8,128)} %reduce-scatter.2.cloned.1.call-done) | non-fusion elementwise | flops 2097152 | bytes 12582912 | tf_op jit(solution)/shard_map/convert_element_type | solution.py:48
  179.6 2.1 convolution_bitcast_fusion.3
  181.7 1.5 convolution_bitcast_fusion.9
  183.1 1.5 convolution_bitcast_fusion.10
  184.6 1.5 convolution_bitcast_fusion.8
  186.1 1.5 convolution_bitcast_fusion.11
  190.1 0.9 bitcast_convert_fusion.1
  190.9 1.1 add_reduce_fusion.1
  192.1 1.1 add_reduce_fusion
  198.0 2.5 %add_reduce_fusion.14 = (f32[]{:T(128)}, f32[]{:T(128)}, f32[]{:T(128)}, f32[]{:T(128)}, f32[]{:T(128)}, /*index=5*/f32[]{:T(128)}, f32[]{:T(128)}, f32[]{:T(128)}) fusion(f32[2,256,256]{2,1,0:T(8,128)} %get-tuple-element.106, f32[256,2,256]{2,0,1:T(8,128)} %bitcast_convert_fusion.2, f32[2,256,256]{2,1,0:T(8,128)} %get-tuple-element.105, ...), kind=kLoop, calls=%fused_computation.152 | loop fusion | flops 2097144 | bytes 2097184 | tf_op jit(solution)/shard_map/reduce_sum | solution.py:22
  203.1 2.2 add_reduce_fusion.12
  207.9 3.5 %add_reduce_fusion.5 = (f32[]{:T(128)}, f32[]{:T(128)}, f32[]{:T(128)}, f32[]{:T(128)}, f32[512,1,256]{2,0,1:T(8,128)S(1)}) fusion(f32[512,2,256]{2,0,1:T(8,128)} %convolution_bitcast_fusion.9, f32[256,2,1024]{2,0,1:T(8,128)S(1)} %convolution_bitcast_fusion.2, f32[256,2,1024]{2,0,1:T(8,128)} %convolution_bitcast_fusion.3, ...), kind=kLoop, calls=%fused_computation.105 | loop fusion | flops 3276796 | bytes 6815760 | tf_op jit(solution)/shard_map/reduce_sum | solution.py:102
  211.4 1.3 add_reduce_fusion.4
  222.8 2.5 %all-reduce = (f32[1,6]{1,0:T(1,128)S(1)}, f32[1,6]{1,0:T(1,128)S(1)}) all-reduce(f32[1,6]{1,0:T(1,128)S(1)} %bitcast.390, f32[1,6]{1,0:T(1,128)S(1)} %bitcast.391), channel_id=1, replica_groups=mesh['grp'=2,'tp'=8,'rb'=2] {'rb'}, use_global_device_ids=true, to_apply=%region_34.35 | all-reduce | flops 12 | bytes 96 | tf_op jit(solution)/shard_map/psum | solution.py:130
  (70 shorter events, 15.5 us)
Async XLA Ops:
  6.5 164.1 %reduce-scatter.2.cloned.1.call-start = ((), (), s32[]{:S(2)}) async-start(), calls=%async_computation.2 | async-start | bytes 25165824 | tf_op jit(solution)/shard_map/reduce_scatter | solution.py:39
  143.9 0.7 copy-start.8
  143.9 8.7 %copy-start.4 = (bf16[7,2,256,256]{3,2,1,0:T(8,128)(2,1)S(1)}, bf16[7,2,256,256]{3,2,1,0:T(8,128)(2,1)}, u32[]{:S(2)}) copy-start(bf16[7,2,256,256]{3,2,1,0:T(8,128)(2,1)} %param.6) | copy-start | bytes 5505028
  174.9 1.5 copy-start.5
  178.8 2.8 %copy-start.6 = (bf16[1,256,2,256]{1,3,2,0:T(8,128)(2,1)S(1)}, bf16[1,256,2,256]{1,3,2,0:T(8,128)(2,1)}, u32[]{:S(2)}) copy-start(bf16[1,256,2,256]{1,3,2,0:T(8,128)(2,1)} %get-tuple-element.89) | copy-start | bytes 786436
  178.8 2.8 %copy-start.7 = (bf16[1,256,2,256]{1,3,2,0:T(8,128)(2,1)S(1)}, bf16[1,256,2,256]{1,3,2,0:T(8,128)(2,1)}, u32[]{:S(2)}) copy-start(bf16[1,256,2,256]{1,3,2,0:T(8,128)(2,1)} %get-tuple-element.90) | copy-start | bytes 786436
  192.1 11.1 %copy-start.1 = (f32[2,256,256]{2,1,0:T(8,128)S(1)}, f32[2,256,256]{2,1,0:T(8,128)}, u32[]{:S(2)}) copy-start(f32[2,256,256]{2,1,0:T(8,128)} %get-tuple-element.108) | copy-start | bytes 1572868
  205.3 6.1 %copy-start.2 = (f32[512,2,256]{2,0,1:T(8,128)S(1)}, f32[512,2,256]{2,0,1:T(8,128)}, u32[]{:S(2)}) copy-start(f32[512,2,256]{2,0,1:T(8,128)} %convolution_bitcast_fusion.8) | copy-start | bytes 3145732
  207.9 3.5 %copy-start = (f32[256,2,1024]{2,0,1:T(8,128)S(1)}, f32[256,2,1024]{2,0,1:T(8,128)}, u32[]{:S(2)}) copy-start(f32[256,2,1024]{2,0,1:T(8,128)} %convolution_bitcast_fusion.3) | copy-start | bytes 6291460
  207.9 3.5 %copy-start.3 = (f32[512,2,256]{2,0,1:T(8,128)S(1)}, f32[512,2,256]{2,0,1:T(8,128)}, u32[]{:S(2)}) copy-start(f32[512,2,256]{2,0,1:T(8,128)} %convolution_bitcast_fusion.11) | copy-start | bytes 3145732
Sparse Core Ops, SparseCore 0:
  144.0 26.6 reduce-scatter.1
where the time goes:
time: 235 us; the launch traced here: 233 us
  blocking collectives  99.3 us (42%)
  between operations  41.8 us (18%)
  other arithmetic  34.3 us (15%)
  local copies, waits for them, and re-layouts  23.6 us (10%)
  matrix products  21.1 us (9%)
  waiting for transfers between devices  12.9 us (5%)
    all_to_all x1, blocking collectives, shards(): lax.all_to_all(picked, 'tp', split_axis=1, concat_axis=0, tiled=True)  96.9 us
    gather x2, local copies, waits for them, and re-layouts, shards(): picked = jnp.take(peram, owner_times, axis=1)  18.6 us
    reduce_scatter x1, waiting for transfers between devices, shards(): lax.psum_scatter(jnp.stack([contract_rows(factor[:, time_slot], right_pai...  12.9 us
    dot_general x2, matrix products, contract_rows(): lax.dot_general(left_rows, right_pair, (((1, 2), (2, 3)), ((), ())), pref...  9.05 us
    dot_general x8, matrix products, shards(): lax.dot_general(col_block, right_four, (((1, 2), (0, 1)), ((), ())), pref...  7.77 us
    reduce_sum x4, other arithmetic, shards(): jnp.sum(product[:, 0] * partner[:, 1] + product[:, 1] * partner[:, 0])  7.01 us
    another operation x1, other arithmetic, shards(): jnp.stack([contract_rows(factor[:, time_slot], right_pairs[time_slot]) fo...  6.57 us
  transfers between devices with their start and end apart: 1, of which 1 were waited for; matrix products, arithmetic and copies ran while one was open for 2% of the time, Pallas kernels for 0%

commit v1 on v0

v1 whole, which is shorter than its diff:
```python
import functools

import jax
import jax.numpy as jnp
from jax import lax
from jax.experimental import pallas as pl
from jax.experimental.pallas import tpu as pltpu
from jax.sharding import PartitionSpec as P

MESH = pl.DeviceIdType.MESH


def gather_kernel(
    owners, diags, times_ref, mom_ref, peram_ref, elems_ref, picked_ref, esel_ref,
    stage, estage, in_sem, out_sem, ein_sem, eout_sem
):
    def load(item):
        slot, owner = lax.rem(item, 2), lax.div(item, 2)
        return pltpu.make_async_copy(
            peram_ref.at[:, times_ref[owner, slot]], stage.at[slot, owner], in_sem.at[slot, owner]
        )

    def save(item):
        slot, owner = lax.rem(item, 2), lax.div(item, 2)
        return pltpu.make_async_copy(
            stage.at[slot, owner], picked_ref.at[slot, owner], out_sem.at[slot, owner]
        )

    def elem_load(item):
        return pltpu.make_async_copy(
            elems_ref.at[mom_ref[0, item // 2, item % 2]], estage.at[item], ein_sem.at[item]
        )

    def elem_save(item):
        return pltpu.make_async_copy(estage.at[item], esel_ref.at[item], eout_sem.at[item])

    def each(total, step):
        def body(item, carry):
            step(item)
            return carry

        lax.fori_loop(0, total, body, 0)

    each(2 * owners, lambda item: load(item).start())
    for item in range(2 * diags):
        elem_load(item).start()

    def forward(item):
        load(item).wait()
        save(item).start()

    each(2 * owners, forward)
    for item in range(2 * diags):
        elem_load(item).wait()
        elem_save(item).start()
    each(2 * owners, lambda item: save(item).wait())
    for item in range(2 * diags):
        elem_save(item).wait()


def dot_nt(left, right):
    return lax.dot_general(
        left, right, (((1,), (1,)), ((), ())), preferred_element_type=jnp.float32
    )


def dot_nn(left, right):
    return lax.dot_general(
        left, right, (((1,), (0,)), ((), ())), preferred_element_type=jnp.float32
    )


def fold(values):
    rows, cols = values.shape
    return jnp.sum(values.reshape(rows // 8, 8, cols), axis=0)


def main_kernel(
    n, nspin, diags, picked_ref, esel_ref, out_ref,
    recv, factor, elems, right4, left3, acc, mine, theirs,
    send_sem, recv_sem, fwd_send, fwd_recv, own_sem, own_send, own_recv, elem_sem, x_sem
):
    me = lax.axis_index("tp")
    core = lax.axis_index("rb")
    other = 1 - core
    rows, sinks = recv.shape[3], recv.shape[5]
    nv = elems.shape[-1]
    per_spin = n // nspin
    my_spin = me // per_spin
    my_place = me % per_spin

    barrier = pltpu.get_barrier_semaphore()

    def greet(step, carry):
        peer = (me + step) % n
        for target in range(2):
            pl.semaphore_signal(barrier, inc=1, device_id={"tp": peer, "rb": target}, device_id_type=MESH)
        return carry

    lax.fori_loop(1, n, greet, 0)
    pl.semaphore_signal(barrier, inc=1, device_id={"rb": other}, device_id_type=MESH)
    pl.semaphore_wait(barrier, 2 * n - 1)

    def group_at(phase):
        if nspin == 4:
            swap = my_spin + 1 - 2 * (my_spin % 2)
            far = (my_spin + 2) % 4
            last = 3 - my_spin
            return jnp.where(phase == 0, my_spin, jnp.where(phase == 1, swap, jnp.where(phase == 2, far, last)))
        return (my_spin + phase) % nspin

    def send(peer, slot):
        return pltpu.make_async_remote_copy(
            src_ref=picked_ref.at[slot, peer],
            dst_ref=recv.at[slot, me, core],
            send_sem=send_sem.at[slot, peer],
            recv_sem=recv_sem.at[me, core],
            device_id={"tp": peer, "rb": slot},
            device_id_type=MESH,
        )

    def arrival(source, half):
        return pltpu.make_async_remote_copy(
            src_ref=recv.at[core, source, half],
            dst_ref=recv.at[core, source, half],
            send_sem=send_sem.at[0, source],
            recv_sem=recv_sem.at[source, half],
            device_id={"rb": other},
            device_id_type=MESH,
        )

    def forward(slot, source, half):
        return pltpu.make_async_remote_copy(
            src_ref=recv.at[slot, source, half],
            dst_ref=recv.at[slot, source, half],
            send_sem=fwd_send.at[source, half],
            recv_sem=fwd_recv.at[source, half],
            device_id={"rb": other},
            device_id_type=MESH,
        )

    def own_local(slot):
        return pltpu.make_async_copy(picked_ref.at[slot, me], recv.at[slot, me, core], own_sem.at[slot])

    def own_remote(slot, half):
        return pltpu.make_async_remote_copy(
            src_ref=picked_ref.at[slot, me],
            dst_ref=recv.at[slot, me, half],
            send_sem=own_send.at[slot],
            recv_sem=own_recv.at[slot],
            device_id={"rb": other},
            device_id_type=MESH,
        )

    def start_phase(phase, carry):
        group = group_at(phase)

        def start_peer(step, inner):
            peer = group * per_spin + (my_place + step) % per_spin

            @pl.when(peer != me)
            def _():
                for slot in range(2):
                    send(peer, slot).start()

            return inner

        return lax.fori_loop(0, per_spin, start_peer, carry)

    lax.fori_loop(0, nspin, start_phase, 0)
    for slot in range(2):
        own_local(slot).start()
        own_remote(slot, core).start()
    elem_copy = pltpu.make_async_copy(esel_ref, elems, elem_sem)
    elem_copy.start()

    acc[...] = jnp.zeros_like(acc)
    elem_copy.wait()
    for d in range(diags):
        three_re = elems[2 * d, 0].astype(jnp.float32).T.astype(jnp.bfloat16)
        three_im = elems[2 * d, 1].astype(jnp.float32).T.astype(jnp.bfloat16)
        base = 2 * nv * d
        left3[base : base + nv, :nv] = three_re
        left3[base : base + nv, nv:] = three_im
        left3[base + nv : base + 2 * nv, :nv] = three_im
        left3[base + nv : base + 2 * nv, nv:] = -three_re
        right4[:nv, base : base + nv] = elems[2 * d + 1, 0]
        right4[:nv, base + nv : base + 2 * nv] = elems[2 * d + 1, 1]
        right4[nv:, base : base + nv] = -elems[2 * d + 1, 1]
        right4[nv:, base + nv : base + 2 * nv] = elems[2 * d + 1, 0]

    def unpack(slot, phase, source, place, half):
        planes = jnp.swapaxes(recv[slot, source, half], 0, 1)
        at = pl.ds(pl.multiple_of(place * rows, rows), rows)
        factor[slot, phase, at, half * sinks : (half + 1) * sinks] = planes[0]
        factor[slot, phase, at, (2 + half) * sinks : (3 + half) * sinks] = planes[1]

    def add_cross(product, partner):
        for d in range(diags):
            base = 2 * nv * d
            p_re, p_im = product[:, base : base + nv], product[:, base + nv : base + 2 * nv]
            q_re, q_im = partner[base : base + nv], partner[base + nv : base + 2 * nv]
            acc[6 * d] += fold(p_re * q_re - p_im * q_im)
            acc[6 * d + 1] += fold(p_re * q_im + p_im * q_re)

    def add_direct(d, which, block_re, block_im):
        e_re = elems[2 * d + which, 0].astype(jnp.float32)
        e_im = elems[2 * d + which, 1].astype(jnp.float32)
        acc[6 * d + 2 + 2 * which] += fold(e_re * block_re + e_im * block_im)
        acc[6 * d + 3 + 2 * which] += fold(e_im * block_re - e_re * block_im)

    def gram(slot, row, col):
        cut = 2 * sinks
        left, right = factor[slot, row], factor[slot, col]
        real = dot_nt(left, right)
        imag = dot_nt(left[:, :cut], right[:, cut:]) - dot_nt(left[:, cut:], right[:, :cut])
        return real.astype(jnp.bfloat16), imag.astype(jnp.bfloat16)

    def run_pair(row, col):
        a_re, a_im = gram(0, row, col)
        b_re, b_im = gram(1, row, col)
        product = dot_nn(b_re, right4[:nv]) + dot_nn(b_im, right4[nv:])
        partner = dot_nn(left3[:, :nv], a_re) + dot_nn(left3[:, nv:], a_im)
        add_cross(product, partner)
        wide = [value.astype(jnp.float32) for value in (a_re, a_im, b_re, b_im)]

        @pl.when(row != col)
        def _():
            flip_re = wide[2].T.astype(jnp.bfloat16)
            flip_im = wide[3].T.astype(jnp.bfloat16)
            product = dot_nn(flip_re, right4[:nv]) - dot_nn(flip_im, right4[nv:])
            partner = dot_nt(left3[:, :nv], a_re) - dot_nt(left3[:, nv:], a_im)
            add_cross(product, partner)

        @pl.when(row == col)
        def _():
            for d in range(diags):
                add_direct(d, 0, wide[0], wide[1])
                add_direct(d, 1, wide[2], wide[3])

    def run_phase(phase, carry):
        group = group_at(phase)

        @pl.when(phase == 0)
        def _():
            for slot in range(2):
                own_local(slot).wait()
                own_remote(slot, other).wait_recv()

        def take(place, inner):
            source = group * per_spin + place
            for half in range(2):

                @pl.when(source != me)
                def _():
                    arrival(source, half).wait_recv()
                    forward(core, source, half).start()

                unpack(core, phase, source, place, half)
            return inner

        lax.fori_loop(0, per_spin, take, 0)

        def take_forwarded(place, inner):
            source = group * per_spin + place
            for half in range(2):

                @pl.when(source != me)
                def _():
                    forward(other, source, half).wait_recv()

                unpack(other, phase, source, place, half)
            return inner

        lax.fori_loop(0, per_spin, take_forwarded, 0)

        def pair(step, inner):
            run_pair(phase, 2 * step + core)
            return inner

        return lax.fori_loop(0, (phase - core + 2) // 2, pair, carry)

    lax.fori_loop(0, nspin, run_phase, 0)

    half_lanes = nv // 2
    total = jnp.sum(acc[...], axis=1)
    mine[...] = total[:, :half_lanes] + total[:, half_lanes:]
    swap = pltpu.make_async_remote_copy(
        src_ref=mine,
        dst_ref=theirs,
        send_sem=x_sem.at[0],
        recv_sem=x_sem.at[1],
        device_id={"rb": other},
        device_id_type=MESH,
    )
    swap.start()

    def finish(step, carry):
        peer = (me + step) % n
        for slot in range(2):
            send(peer, slot).wait_send()
            forward(core, peer, slot).wait_send()
        return carry

    lax.fori_loop(1, n, finish, 0)
    for slot in range(2):
        own_remote(slot, core).wait_send()
    swap.wait()
    out_ref[...] = mine[...] + theirs[...]


def shards(peram, src_elems, owner_times, diag_mom, diag_count):
    n = lax.axis_size("tp")
    rows, _, parts, sinks = peram.shape
    nv = src_elems.shape[-1]
    nspin = n * rows // nv
    diags = diag_mom.shape[1]
    bf16, f32 = jnp.bfloat16, jnp.float32
    any_spec = pl.BlockSpec(memory_space=pl.ANY)
    smem_spec = pl.BlockSpec(memory_space=pltpu.SMEM)
    dma = pltpu.SemaphoreType.DMA
    picked, chosen = pl.pallas_call(
        functools.partial(gather_kernel, n, diags),
        out_shape=(
            jax.ShapeDtypeStruct((2, n, rows, parts, sinks), bf16),
            jax.ShapeDtypeStruct((2 * diags, 2, nv, nv), bf16),
        ),
        in_specs=[smem_spec, smem_spec, any_spec, any_spec],
        out_specs=(any_spec, any_spec),
        scratch_shapes=[
            pltpu.VMEM((2, n, rows, parts, sinks), bf16),
            pltpu.VMEM((2 * diags, 2, nv, nv), bf16),
            dma((2, n)), dma((2, n)), dma((2 * diags,)), dma((2 * diags,)),
        ],
        name="pick",
    )(owner_times, diag_mom, peram, src_elems)
    sums = 6 * diags
    lanes = nv // 2
    values = pl.pallas_call(
        functools.partial(main_kernel, n, nspin, diags),
        out_shape=jax.ShapeDtypeStruct((sums, lanes), f32),
        in_specs=[any_spec, any_spec],
        out_specs=pl.BlockSpec(memory_space=pltpu.VMEM),
        scratch_shapes=[
            pltpu.VMEM((2, n, 2, rows, parts, sinks), bf16),
            pltpu.VMEM((2, nspin, nv, 4 * sinks), bf16),
            pltpu.VMEM((2 * diags, 2, nv, nv), bf16),
            pltpu.VMEM((2 * nv, 2 * diags * nv), bf16),
            pltpu.VMEM((2 * diags * nv, 2 * nv), bf16),
            pltpu.VMEM((sums, 8, nv), f32),
            pltpu.VMEM((sums, lanes), f32),
            pltpu.VMEM((sums, lanes), f32),
            dma((2, n)), dma((n, 2)), dma((n, 2)), dma((n, 2)),
            dma((2,)), dma((2,)), dma((2,)), dma, dma((2,)),
        ],
        compiler_params=pltpu.CompilerParams(collective_id=0, has_side_effects=True),
        name="contract",
    )(picked, chosen)
    stacked = jnp.sum(values, axis=1).reshape(diags, 6)
    direct_re = stacked[:, 2] * stacked[:, 4] - stacked[:, 3] * stacked[:, 5]
    direct_im = stacked[:, 2] * stacked[:, 5] + stacked[:, 3] * stacked[:, 4]
    direct = jnp.stack([direct_re, direct_im], axis=-1)
    values_all = 0.25 * jnp.stack([direct, stacked[:, 0:2]], axis=1)
    keep = (jnp.arange(diags, dtype=jnp.int32) < diag_count[0])[:, None, None]
    return jnp.where(keep, values_all, jnp.zeros_like(values_all))[None]


def solution(mesh):
    in_specs = (
        P(("grp", "tp"), None, None, "rb"),
        P("grp", None, None, None),
        P("grp", None),
        P(("grp", "tp"), None, None),
        P(("grp", "tp")),
    )
    out_specs = P(("grp", "tp"), None, None, None)
    return jax.shard_map(shards, mesh=mesh, in_specs=in_specs, out_specs=out_specs, check_vma=False)
```

time: 235 us -> 115 us (0.49)
  Pallas kernels: 0 us -> 110 us
  blocking collectives: 99.3 us -> 0 us
  between operations: 41.8 us -> 0.68 us
  other arithmetic: 34.3 us -> 1.05 us
  local copies, waits for them, and re-layouts: 23.6 us -> 2.01 us
  matrix products: 21.1 us -> 0 us
  waiting for transfers between devices: 12.9 us -> 0 us
    pallas_call x0 -> x2, Pallas kernels: none -> 110 us  [the longest x1 105 us: shards(): pl.pallas_call(functools.partial(main_kernel, n, nspin, diags), out_shape...]
    all_to_all x1 -> x0, blocking collectives: 96.9 us -> none  [shards(): lax.all_to_all(picked, 'tp', split_axis=1, concat_axis=0, tiled=True)]
    dot_general x14 -> x0, matrix products: 21.1 us -> none  [the longest x2 9.05 us: contract_rows(): lax.dot_general(left_rows, right_pair, (((1, 2), (2, 3)), ((), ())), pref...]
    gather x2 -> x0, local copies, waits for them, and re-layouts: 18.6 us -> none  [shards(): picked = jnp.take(peram, owner_times, axis=1)]
    reduce_scatter x1 -> x0, waiting for transfers between devices: 12.9 us -> none  [shards(): lax.psum_scatter(jnp.stack([contract_rows(factor[:, time_slot], right_pai...]
    reduce_sum x6 -> x1, other arithmetic: 11.6 us -> 0.81 us  [shards(): stacked = jnp.sum(values, axis=1).reshape(diags, 6)]
    convert_element_type x7 -> x0, other arithmetic: 9.46 us -> none  [the longest x1 4.04 us: shards(): meson_rows = summed.astype(jnp.bfloat16)]
    another operation x9 -> x1, other arithmetic: 8.73 us -> 0.08 us  [shards(): values_all = 0.25 * jnp.stack([direct, stacked[:, 0:2]], axis=1)]
  transfers between devices with their start and end apart: 1 -> 0, of which waited for: 1 -> 0; matrix products, arithmetic and copies ran while one was open for 2% -> 0% of each run, Pallas kernels for 0% -> 0%
where the time goes in v1:
time: 115 us; the launch traced here: 114 us
  Pallas kernels  110 us (96%)
  local copies, waits for them, and re-layouts  2.01 us (2%)
    pallas_call x1, Pallas kernels, shards(): pl.pallas_call(functools.partial(main_kernel, n, nspin, diags), out_shape...  105 us
    pallas_call x1, Pallas kernels, shards(): pl.pallas_call(functools.partial(gather_kernel, n, diags), out_shape=(jax...  5.78 us

profile of v1, /device:TPU:9, one launch (start us, length us, event | category | flops | bytes accessed | tf_op | source)
XLA Modules:
  0.0 114.2 jit_solution(9962274578047207864)
XLA Ops:
  0.0 1.3 %copy.6.times_ref = s32[8,2]{1,0:T(8,128)} copy(s32[8,2]{0,1:T(2,128)} %param.7) | data formatting | bytes 128 | tf_op args[2]
  1.3 5.8 %pick.1 = (bf16[2,8,128,2,512]{4,3,2,1,0:T(2,128)(2,1)}, bf16[4,2,256,256]{3,2,1,0:T(8,128)(2,1)}) custom-call(s32[8,2]{1,0:T(8,128)} %copy.6.times_ref, s32[1,2,2]{2,1,0:T(2,128)} %mom_ref.1, bf16[128,24,2,512]{3,2,1,0:T(2,128)(2,1)} %peram_ref.1, bf16[7,2,256,256]{3,2,1,0:T(8,128)(2,1)} %elems_ref.1), custom_call_target="tpu_custom_call" | custom-call | tf_op jit(solution)/shard_map/pick/pallas_call | solution.py:322
  7.1 104.7 %contract.1 = f32[12,128]{1,0:T(8,128)} custom-call(bf16[2,8,128,2,512]{4,3,2,1,0:T(2,128)(2,1)} %get-tuple-element.7.picked_ref, bf16[4,2,256,256]{3,2,1,0:T(8,128)(2,1)} %get-tuple-element.8.esel_ref), custom_call_target="tpu_custom_call" | custom-call | tf_op jit(solution)/shard_map/contract/pallas_call | solution.py:339
  111.9 0.8 reduce_sum.9
  112.7 0.1 reshape.41
  112.8 0.1 multiply_subtract_fusion
  112.8 0.1 maximum_bitcast_fusion
  113.6 0.1 fusion
  113.6 0.6 copy.7
  (1 shorter events, 0.0 us)

commit v2 on v1

v2 whole, which is shorter than its diff:
```python
import functools

import jax
import jax.numpy as jnp
from jax import lax
from jax.experimental import pallas as pl
from jax.experimental.pallas import tpu as pltpu
from jax.sharding import PartitionSpec as P

MESH = pl.DeviceIdType.MESH


def dot_nt(left, right):
    return lax.dot_general(
        left, right, (((1,), (1,)), ((), ())), preferred_element_type=jnp.float32
    )


def dot_nn(left, right):
    return lax.dot_general(
        left, right, (((1,), (0,)), ((), ())), preferred_element_type=jnp.float32
    )


def fold(values):
    rows, cols = values.shape
    return jnp.sum(values.reshape(rows // 8, 8, cols), axis=0)


def main_kernel(
    n, nspin, diags, times_hbm, mom_hbm, count_hbm, peram_ref, elems_ref, out_ref,
    slab, packed, recv, elems, right4, left3, acc, mine, theirs, times, mom, count,
    slab_sem, small_sem, elem_sem, send_sem, recv_sem, fwd_send, fwd_recv, own_send, own_recv, x_sem
):
    me = lax.axis_index("tp")
    core = lax.axis_index("rb")
    other = 1 - core
    rows, sinks = packed.shape[3], packed.shape[4]
    nv = elems.shape[-1]
    per_spin = n // nspin
    my_spin = me // per_spin
    my_place = me % per_spin

    pieces = slab_sem.shape[0]
    cut_rows = rows // pieces
    slab_copies = [
        pltpu.make_async_copy(
            peram_ref.at[pl.ds(i * cut_rows, cut_rows)], slab.at[pl.ds(i * cut_rows, cut_rows)], slab_sem.at[i]
        )
        for i in range(pieces)
    ]
    small_copies = [
        pltpu.make_async_copy(times_hbm, times, small_sem.at[0]),
        pltpu.make_async_copy(mom_hbm, mom, small_sem.at[1]),
        pltpu.make_async_copy(count_hbm, count, small_sem.at[2]),
    ]
    elem_copy = pltpu.make_async_copy(elems_ref, elems, elem_sem)
    for copy in small_copies + slab_copies:
        copy.start()
    elem_copy.start()

    barrier = pltpu.get_barrier_semaphore()

    def greet(step, carry):
        peer = (me + step) % n
        for target in range(2):
            pl.semaphore_signal(barrier, inc=1, device_id={"tp": peer, "rb": target}, device_id_type=MESH)
        return carry

    lax.fori_loop(1, n, greet, 0)
    pl.semaphore_signal(barrier, inc=1, device_id={"rb": other}, device_id_type=MESH)

    def group_at(phase):
        if nspin == 4:
            swap = my_spin + 1 - 2 * (my_spin % 2)
            far = (my_spin + 2) % 4
            last = 3 - my_spin
            return jnp.where(phase == 0, my_spin, jnp.where(phase == 1, swap, jnp.where(phase == 2, far, last)))
        return (my_spin + phase) % nspin

    def send_phase(step):
        if nspin == 4:
            inner = jnp.where(step == 0, 2, jnp.where(step == 1, 3, jnp.where(step == 2, 1, 0)))
            outer = (step + 1) % 4
            return jnp.where(((my_spin + 1) // 2) % 2 == 1, inner, outer)
        return (step + 1) % nspin

    def landing(slot, source, half):
        return recv.at[
            slot,
            :,
            pl.ds(pl.multiple_of(source * rows, rows), rows),
            pl.ds(pl.multiple_of(half * sinks, sinks), sinks),
        ]

    def send(peer, slot):
        return pltpu.make_async_remote_copy(
            src_ref=packed.at[slot, peer],
            dst_ref=landing(slot, me, core),
            send_sem=send_sem.at[slot, peer],
            recv_sem=recv_sem.at[me, core],
            device_id={"tp": peer, "rb": slot},
            device_id_type=MESH,
        )

    def arrival(source, half):
        return pltpu.make_async_remote_copy(
            src_ref=landing(core, source, half),
            dst_ref=landing(core, source, half),
            send_sem=send_sem.at[0, source],
            recv_sem=recv_sem.at[source, half],
            device_id={"rb": other},
            device_id_type=MESH,
        )

    def forward(slot, source, half):
        return pltpu.make_async_remote_copy(
            src_ref=landing(slot, source, half),
            dst_ref=landing(slot, source, half),
            send_sem=fwd_send.at[source, half],
            recv_sem=fwd_recv.at[source, half],
            device_id={"rb": other},
            device_id_type=MESH,
        )

    def own(slot, half):
        return pltpu.make_async_remote_copy(
            src_ref=landing(slot, me, half),
            dst_ref=landing(slot, me, half),
            send_sem=own_send.at[slot],
            recv_sem=own_recv.at[slot],
            device_id={"rb": other},
            device_id_type=MESH,
        )

    def peer_at(step):
        group = group_at(send_phase(step // per_spin))
        return group * per_spin + (my_place + step % per_spin) % per_spin

    for copy in small_copies + slab_copies:
        copy.wait()

    def planes_of(peer, slot):
        return jnp.swapaxes(slab[:, times[peer, slot]], 0, 1)

    def build(step):
        peer = peer_at(step)
        for slot in range(2):
            packed[slot, peer] = planes_of(peer, slot)

    def launch(step):
        peer = peer_at(step)

        @pl.when(peer != me)
        def _():
            for slot in range(2):
                send(peer, slot).start()

    build(0)
    pl.semaphore_wait(barrier, 2 * n - 1)

    def build_and_launch(step, carry):
        build(step)
        launch(step - 1)
        return carry

    lax.fori_loop(1, n, build_and_launch, 0)
    for slot in range(2):
        planes = planes_of(me, slot)
        at = pl.ds(pl.multiple_of(me * rows, rows), rows)
        recv[slot, :, at, pl.ds(pl.multiple_of(core * sinks, sinks), sinks)] = planes
    launch(n - 1)

    acc[...] = jnp.zeros_like(acc)
    elem_copy.wait()
    for d in range(diags):
        elem3, elem4 = elems[mom[0, d, 0]], elems[mom[0, d, 1]]
        three_re = elem3[0].astype(jnp.float32).T.astype(jnp.bfloat16)
        three_im = elem3[1].astype(jnp.float32).T.astype(jnp.bfloat16)
        base = 2 * nv * d
        left3[base : base + nv, :nv] = three_re
        left3[base : base + nv, nv:] = three_im
        left3[base + nv : base + 2 * nv, :nv] = three_im
        left3[base + nv : base + 2 * nv, nv:] = -three_re
        right4[:nv, base : base + nv] = elem4[0]
        right4[:nv, base + nv : base + 2 * nv] = elem4[1]
        right4[nv:, base : base + nv] = -elem4[1]
        right4[nv:, base + nv : base + 2 * nv] = elem4[0]
    for slot in range(2):
        own(slot, core).start()

    def add_cross(product, partner):
        for d in range(diags):
            base = 2 * nv * d
            p_re, p_im = product[:, base : base + nv], product[:, base + nv : base + 2 * nv]
            q_re, q_im = partner[base : base + nv], partner[base + nv : base + 2 * nv]
            acc[6 * d] += fold(p_re * q_re - p_im * q_im)
            acc[6 * d + 1] += fold(p_re * q_im + p_im * q_re)

    def add_direct(d, which, block_re, block_im):
        elem = elems[mom[0, d, which]].astype(jnp.float32)
        e_re, e_im = elem[0], elem[1]
        acc[6 * d + 2 + 2 * which] += fold(e_re * block_re + e_im * block_im)
        acc[6 * d + 3 + 2 * which] += fold(e_im * block_re - e_re * block_im)

    def gram(slot, row, col):
        def part(index, spin):
            return recv[slot, index, pl.ds(pl.multiple_of(spin * nv, nv), nv), :]

        left_re, left_im, right_re, right_im = part(0, row), part(1, row), part(0, col), part(1, col)
        real = dot_nt(left_re, right_re) + dot_nt(left_im, right_im)
        imag = dot_nt(left_re, right_im) - dot_nt(left_im, right_re)
        return real.astype(jnp.bfloat16), imag.astype(jnp.bfloat16)

    def run_pair(row, col):
        a_re, a_im = gram(0, row, col)
        b_re, b_im = gram(1, row, col)
        product = dot_nn(b_re, right4[:nv]) + dot_nn(b_im, right4[nv:])
        partner = dot_nn(left3[:, :nv], a_re) + dot_nn(left3[:, nv:], a_im)
        add_cross(product, partner)
        wide = [value.astype(jnp.float32) for value in (a_re, a_im, b_re, b_im)]

        @pl.when(row != col)
        def _():
            flip_re = wide[2].T.astype(jnp.bfloat16)
            flip_im = wide[3].T.astype(jnp.bfloat16)
            product = dot_nn(flip_re, right4[:nv]) - dot_nn(flip_im, right4[nv:])
            partner = dot_nt(left3[:, :nv], a_re) - dot_nt(left3[:, nv:], a_im)
            add_cross(product, partner)

        @pl.when(row == col)
        def _():
            for d in range(diags):
                add_direct(d, 0, wide[0], wide[1])
                add_direct(d, 1, wide[2], wide[3])

    def run_phase(phase, carry):
        group = group_at(phase)

        @pl.when(phase == 0)
        def _():
            for slot in range(2):
                own(slot, other).wait_recv()

        def source_at(step):
            return group * per_spin + (my_place + per_spin - step) % per_spin

        def take(step, inner):
            source = source_at(step)

            @pl.when(source != me)
            def _():
                for half in range(2):
                    arrival(source, half).wait_recv()
                    forward(core, source, half).start()

            return inner

        lax.fori_loop(0, per_spin, take, 0)

        def take_forwarded(step, inner):
            source = source_at(step)

            @pl.when(source != me)
            def _():
                for half in range(2):
                    forward(other, source, half).wait_recv()

            return inner

        lax.fori_loop(0, per_spin, take_forwarded, 0)

        def pair(step, inner):
            run_pair(group, group_at(2 * step + core))
            return inner

        return lax.fori_loop(0, (phase - core + 2) // 2, pair, carry)

    lax.fori_loop(0, nspin, run_phase, 0)

    half_lanes = nv // 2
    total = jnp.sum(acc[...], axis=1)
    mine[...] = total[:, :half_lanes] + total[:, half_lanes:]

    def finish(step, carry):
        peer = (me + step) % n
        for slot in range(2):
            send(peer, slot).wait_send()
            forward(core, peer, slot).wait_send()
        return carry

    lax.fori_loop(1, n, finish, 0)
    for slot in range(2):
        own(slot, core).wait_send()
    swap = pltpu.make_async_remote_copy(
        src_ref=mine,
        dst_ref=theirs,
        send_sem=x_sem.at[0],
        recv_sem=x_sem.at[1],
        device_id={"rb": other},
        device_id_type=MESH,
    )
    swap.start()
    swap.wait()
    both = mine[...] + theirs[...]
    for d in range(diags):
        c_re, c_im, t_re, t_im, f_re, f_im = (jnp.sum(both[6 * d + i : 6 * d + i + 1]) for i in range(6))
        used = d < count[0]
        line = (t_re * f_re - t_im * f_im, t_re * f_im + t_im * f_re, c_re, c_im)
        for i, value in enumerate(line):
            out_ref[4 * d + i] = jnp.where(used, 0.25 * value, 0.0)


def shards(peram, src_elems, owner_times, diag_mom, diag_count):
    n = lax.axis_size("tp")
    rows, _, parts, sinks = peram.shape
    nv = src_elems.shape[-1]
    nspin = n * rows // nv
    diags = diag_mom.shape[1]
    bf16, f32 = jnp.bfloat16, jnp.float32
    any_spec = pl.BlockSpec(memory_space=pl.ANY)
    dma = pltpu.SemaphoreType.DMA
    sums = 6 * diags
    lanes = nv // 2
    values = pl.pallas_call(
        functools.partial(main_kernel, n, nspin, diags),
        out_shape=jax.ShapeDtypeStruct((4 * diags,), f32),
        in_specs=[any_spec] * 5,
        out_specs=pl.BlockSpec(memory_space=pltpu.SMEM),
        scratch_shapes=[
            pltpu.VMEM(peram.shape, bf16),
            pltpu.VMEM((2, n, parts, rows, sinks), bf16),
            pltpu.VMEM((2, parts, n * rows, 2 * sinks), bf16),
            pltpu.VMEM(src_elems.shape, bf16),
            pltpu.VMEM((2 * nv, 2 * diags * nv), bf16),
            pltpu.VMEM((2 * diags * nv, 2 * nv), bf16),
            pltpu.VMEM((sums, 8, nv), f32),
            pltpu.VMEM((sums, lanes), f32),
            pltpu.VMEM((sums, lanes), f32),
            pltpu.SMEM(owner_times.shape, jnp.int32),
            pltpu.SMEM(diag_mom.shape, jnp.int32),
            pltpu.SMEM(diag_count.shape, jnp.int32),
            dma((4,)), dma((3,)), dma,
            dma((2, n)), dma((n, 2)), dma((n, 2)), dma((n, 2)), dma((2,)), dma((2,)), dma((2,)),
        ],
        compiler_params=pltpu.CompilerParams(collective_id=0, has_side_effects=True),
        name="contract",
    )(owner_times, diag_mom, diag_count, peram, src_elems)
    return values.reshape(1, diags, 2, 2)


def solution(mesh):
    in_specs = (
        P(("grp", "tp"), None, None, "rb"),
        P("grp", None, None, None),
        P("grp", None),
        P(("grp", "tp"), None, None),
        P(("grp", "tp")),
    )
    out_specs = P(("grp", "tp"), None, None, None)
    return jax.shard_map(shards, mesh=mesh, in_specs=in_specs, out_specs=out_specs, check_vma=False)
```

time: 115 us -> 109 us (0.948)
  Pallas kernels: 110 us -> 106 us
    pallas_call x1 -> x0, Pallas kernels: 5.78 us -> none  [shards(): pl.pallas_call(functools.partial(gather_kernel, n, diags), out_shape=(jax...]
    pallas_call x1, Pallas kernels: 105 us -> 106 us  [shards(): pl.pallas_call(functools.partial(main_kernel, n, nspin, diags), out_shape...]
    reshape x1, local copies, waits for them, and re-layouts: 0.08 us -> 1.26 us  [shards(): return values.reshape(1, diags, 2, 2)]
where the time goes in v2:
time: 109 us
  Pallas kernels  106 us (97%)
  local copies, waits for them, and re-layouts  2.6 us (2%)
    pallas_call x1, Pallas kernels, shards(): pl.pallas_call(functools.partial(main_kernel, n, nspin, diags), out_shape...  106 us

profile of v2, /device:TPU:9, one launch (start us, length us, event | category | flops | bytes accessed | tf_op | source)
XLA Modules:
  0.0 109.2 jit_solution(3781576162726931243)
XLA Ops:
  0.7 1.3 %copy.6.times_hbm = s32[8,2]{1,0:T(8,128)} copy(s32[8,2]{0,1:T(2,128)} %param.7) | data formatting | bytes 128 | tf_op args[2]
  2.0 106.0 %contract.1 = f32[8]{0:T(128)} custom-call(s32[8,2]{1,0:T(8,128)} %copy.6.times_hbm, s32[1,2,2]{2,1,0:T(2,128)} %mom_hbm.1, s32[1]{0:T(128)S(6)} %copy.7.count_hbm, bf16[128,24,2,512]{3,2,1,0:T(2,128)(2,1)} %peram_ref.1, bf16[7,2,256,256]{3,2,1,0:T(8,128)(2,1)} %elems_ref.1), custom_call_target="tpu_custom_call" | custom-call | tf_op jit(solution)/shard_map/contract/pallas_call | solution.py:325
  108.0 1.3 %reshape.3 = f32[1,2,2,2]{3,2,1,0:T(2,128)} reshape(f32[8]{0:T(128)} %contract.1) | data formatting | bytes 64 | tf_op jit(solution)/shard_map/reshape | solution.py:349

commit v3 on v2

--- a/solution.py
+++ b/solution.py
@@ -29,7 +29,7 @@
 
 def main_kernel(
     n, nspin, diags, times_hbm, mom_hbm, count_hbm, peram_ref, elems_ref, out_ref,
-    slab, packed, recv, elems, right4, left3, acc, mine, theirs, times, mom, count,
+    slab, packed, recv, meson, elems, right4, left3, acc, mine, theirs, times, mom, count,
     slab_sem, small_sem, elem_sem, send_sem, recv_sem, fwd_send, fwd_recv, own_send, own_recv, x_sem
 ):
     me = lax.axis_index("tp")
@@ -37,9 +37,17 @@
     other = 1 - core
     rows, sinks = packed.shape[3], packed.shape[4]
     nv = elems.shape[-1]
+    subs = recv_sem.shape[2]
+    sub_rows = rows // subs
     per_spin = n // nspin
     my_spin = me // per_spin
     my_place = me % per_spin
+    early = per_spin // 2
+
+    def place_at(step, sign):
+        return (my_place // early + step // early) % 2 * early + (
+            my_place % early + early + sign * (step % early)
+        ) % early
 
     pieces = slab_sem.shape[0]
     cut_rows = rows // pieces
@@ -85,63 +93,63 @@
             return jnp.where(((my_spin + 1) // 2) % 2 == 1, inner, outer)
         return (step + 1) % nspin
 
-    def landing(slot, source, half):
+    def landing(slot, source, half, sub):
         return recv.at[
             slot,
             :,
-            pl.ds(pl.multiple_of(source * rows, rows), rows),
+            pl.ds(pl.multiple_of(source * rows + sub * sub_rows, sub_rows), sub_rows),
             pl.ds(pl.multiple_of(half * sinks, sinks), sinks),
         ]
 
-    def send(peer, slot):
+    def send(peer, slot, sub):
         return pltpu.make_async_remote_copy(
-            src_ref=packed.at[slot, peer],
-            dst_ref=landing(slot, me, core),
-            send_sem=send_sem.at[slot, peer],
-            recv_sem=recv_sem.at[me, core],
+            src_ref=packed.at[slot, peer, :, pl.ds(sub * sub_rows, sub_rows)],
+            dst_ref=landing(slot, me, core, sub),
+            send_sem=send_sem.at[slot, peer, sub],
+            recv_sem=recv_sem.at[me, core, sub],
             device_id={"tp": peer, "rb": slot},
             device_id_type=MESH,
         )
 
-    def arrival(source, half):
+    def arrival(source, half, sub):
         return pltpu.make_async_remote_copy(
-            src_ref=landing(core, source, half),
-            dst_ref=landing(core, source, half),
-            send_sem=send_sem.at[0, source],
-            recv_sem=recv_sem.at[source, half],
+            src_ref=landing(core, source, half, sub),
+            dst_ref=landing(core, source, half, sub),
+            send_sem=send_sem.at[0, source, sub],
+            recv_sem=recv_sem.at[source, half, sub],
             device_id={"rb": other},
             device_id_type=MESH,
         )
 
-    def forward(slot, source, half):
+    def forward(slot, source, half, sub):
         return pltpu.make_async_remote_copy(
-            src_ref=landing(slot, source, half),
-            dst_ref=landing(slot, source, half),
-            send_sem=fwd_send.at[source, half],
-            recv_sem=fwd_recv.at[source, half],
+            src_ref=landing(slot, source, half, sub),
+            dst_ref=landing(slot, source, half, sub),
+            send_sem=fwd_send.at[source, half, sub],
+            recv_sem=fwd_recv.at[source, half, sub],
             device_id={"rb": other},
             device_id_type=MESH,
         )
 
-    def own(slot, half):
+    def own(slot, half, sub):
         return pltpu.make_async_remote_copy(
-            src_ref=landing(slot, me, half),
-            dst_ref=landing(slot, me, half),
-            send_sem=own_send.at[slot],
-            recv_sem=own_recv.at[slot],
+            src_ref=landing(slot, me, half, sub),
+            dst_ref=landing(slot, me, half, sub),
+            send_sem=own_send.at[slot, sub],
+            recv_sem=own_recv.at[slot, sub],
             device_id={"rb": other},
             device_id_type=MESH,
         )
 
     def peer_at(step):
         group = group_at(send_phase(step // per_spin))
-        return group * per_spin + (my_place + step % per_spin) % per_spin
+        return group * per_spin + place_at(step % per_spin, 1)
 
     for copy in small_copies + slab_copies:
         copy.wait()
 
     def planes_of(peer, slot):
-        return jnp.swapaxes(slab[:, times[peer, slot]], 0, 1)
+        return jnp.swapaxes(slab[:, times[slot, peer]], 0, 1)
 
     def build(step):
         peer = peer_at(step)
@@ -154,7 +162,8 @@
         @pl.when(peer != me)
         def _():
             for slot in range(2):
-                send(peer, slot).start()
+                for sub in range(subs):
+                    send(peer, slot, sub).start()
 
     build(0)
     pl.semaphore_wait(barrier, 2 * n - 1)
@@ -187,7 +196,8 @@
         right4[nv:, base : base + nv] = -elem4[1]
         right4[nv:, base + nv : base + 2 * nv] = elem4[0]
     for slot in range(2):
-        own(slot, core).start()
+        for sub in range(subs):
+            own(slot, core, sub).start()
 
     def add_cross(product, partner):
         for d in range(diags):
@@ -203,24 +213,38 @@
         acc[6 * d + 2 + 2 * which] += fold(e_re * block_re + e_im * block_im)
         acc[6 * d + 3 + 2 * which] += fold(e_im * block_re - e_re * block_im)
 
-    def gram(slot, row, col):
-        def part(index, spin):
-            return recv[slot, index, pl.ds(pl.multiple_of(spin * nv, nv), nv), :]
-
-        left_re, left_im, right_re, right_im = part(0, row), part(1, row), part(0, col), part(1, col)
+    def gram(slot, step, place, start, size, col):
+        def part(index, at, length):
+            return recv[slot, index, pl.ds(pl.multiple_of(at, length), length), :]
+
+        left_re, left_im = part(0, start, size), part(1, start, size)
+        right_re, right_im = part(0, col * nv, nv), part(1, col * nv, nv)
         real = dot_nt(left_re, right_re) + dot_nt(left_im, right_im)
         imag = dot_nt(left_re, right_im) - dot_nt(left_im, right_re)
-        return real.astype(jnp.bfloat16), imag.astype(jnp.bfloat16)
-
-    def run_pair(row, col):
-        a_re, a_im = gram(0, row, col)
-        b_re, b_im = gram(1, row, col)
+        to = pl.ds(pl.multiple_of(place, size), size)
+        meson[slot, step, 0, to] = real.astype(jnp.bfloat16)
+        meson[slot, step, 1, to] = imag.astype(jnp.bfloat16)
+
+    def run_pair(diagonal, step, row, early_place, col):
+        @pl.when(diagonal)
+        def _():
+            for slot in range(2):
+                gram(slot, step, 0, row * nv, nv, col)
+
+        @pl.when(jnp.logical_not(diagonal))
+        def _():
+            place = nv // 2 - early_place
+            for slot in range(2):
+                gram(slot, step, place, row * nv + place, nv // 2, col)
+
+        a_re, a_im = meson[0, step, 0], meson[0, step, 1]
+        b_re, b_im = meson[1, step, 0], meson[1, step, 1]
         product = dot_nn(b_re, right4[:nv]) + dot_nn(b_im, right4[nv:])
         partner = dot_nn(left3[:, :nv], a_re) + dot_nn(left3[:, nv:], a_im)
         add_cross(product, partner)
         wide = [value.astype(jnp.float32) for value in (a_re, a_im, b_re, b_im)]
 
-        @pl.when(row != col)
+        @pl.when(jnp.logical_not(diagonal))
         def _():
             flip_re = wide[2].T.astype(jnp.bfloat16)
             flip_im = wide[3].T.astype(jnp.bfloat16)
@@ -228,7 +252,7 @@
             partner = dot_nt(left3[:, :nv], a_re) - dot_nt(left3[:, nv:], a_im)
             add_cross(product, partner)
 
-        @pl.when(row == col)
+        @pl.when(diagonal)
         def _():
             for d in range(diags):
                 add_direct(d, 0, wide[0], wide[1])
@@ -240,38 +264,51 @@
         @pl.when(phase == 0)
         def _():
             for slot in range(2):
-                own(slot, other).wait_recv()
+                for sub in range(subs):
+                    own(slot, other, sub).wait_recv()
 
         def source_at(step):
-            return group * per_spin + (my_place + per_spin - step) % per_spin
+            return group * per_spin + place_at(step, -1)
 
         def take(step, inner):
             source = source_at(step)
 
             @pl.when(source != me)
             def _():
-                for half in range(2):
-                    arrival(source, half).wait_recv()
-                    forward(core, source, half).start()
+                for sub in range(subs):
+                    for half in range(2):
+                        arrival(source, half, sub).wait_recv()
+                        forward(core, source, half, sub).start()
 
             return inner
-
-        lax.fori_loop(0, per_spin, take, 0)
 
         def take_forwarded(step, inner):
             source = source_at(step)
 
             @pl.when(source != me)
             def _():
-                for half in range(2):
-                    forward(other, source, half).wait_recv()
+                for sub in range(subs):
+                    for half in range(2):
+                        forward(other, source, half, sub).wait_recv()
 
             return inner
 
-        lax.fori_loop(0, per_spin, take_forwarded, 0)
+        early_place = my_place // early * (nv // 2)
+        early_at = group * nv + early_place
+        lax.fori_loop(0, early, take, 0)
+        lax.fori_loop(0, early, take_forwarded, 0)
+
+        def early_rows(step, inner):
+            for slot in range(2):
+                gram(slot, step, early_place, early_at, nv // 2, group_at(2 * step + core))
+            return inner
+
+        lax.fori_loop(0, (phase - core + 1) // 2, early_rows, 0)
+        lax.fori_loop(early, per_spin, take, 0)
+        lax.fori_loop(early, per_spin, take_forwarded, 0)
 
         def pair(step, inner):
-            run_pair(group, group_at(2 * step + core))
+            run_pair(phase == 2 * step + core, step, group, early_place, group_at(2 * step + core))
             return inner
 
         return lax.fori_loop(0, (phase - core + 2) // 2, pair, carry)
@@ -285,13 +322,15 @@
     def finish(step, carry):
         peer = (me + step) % n
         for slot in range(2):
-            send(peer, slot).wait_send()
-            forward(core, peer, slot).wait_send()
+            for sub in range(subs):
+                send(peer, slot, sub).wait_send()
+                forward(core, peer, slot, sub).wait_send()
         return carry
 
     lax.fori_loop(1, n, finish, 0)
     for slot in range(2):
-        own(slot, core).wait_send()
+        for sub in range(subs):
+            own(slot, core, sub).wait_send()
     swap = pltpu.make_async_remote_copy(
         src_ref=mine,
         dst_ref=theirs,
@@ -308,7 +347,7 @@
         used = d < count[0]
         line = (t_re * f_re - t_im * f_im, t_re * f_im + t_im * f_re, c_re, c_im)
         for i, value in enumerate(line):
-            out_ref[4 * d + i] = jnp.where(used, 0.25 * value, 0.0)
+            out_ref[0, d, i // 2, i % 2] = jnp.where(used, 0.25 * value, 0.0)
 
 
 def shards(peram, src_elems, owner_times, diag_mom, diag_count):
@@ -321,32 +360,35 @@
     any_spec = pl.BlockSpec(memory_space=pl.ANY)
     dma = pltpu.SemaphoreType.DMA
     sums = 6 * diags
+    subs = max(1, min(4, rows // 16 // 2))
     lanes = nv // 2
     values = pl.pallas_call(
         functools.partial(main_kernel, n, nspin, diags),
-        out_shape=jax.ShapeDtypeStruct((4 * diags,), f32),
+        out_shape=jax.ShapeDtypeStruct((1, diags, 2, 2), f32),
         in_specs=[any_spec] * 5,
         out_specs=pl.BlockSpec(memory_space=pltpu.SMEM),
         scratch_shapes=[
             pltpu.VMEM(peram.shape, bf16),
             pltpu.VMEM((2, n, parts, rows, sinks), bf16),
             pltpu.VMEM((2, parts, n * rows, 2 * sinks), bf16),
+            pltpu.VMEM((2, nspin // 2, 2, nv, nv), bf16),
             pltpu.VMEM(src_elems.shape, bf16),
             pltpu.VMEM((2 * nv, 2 * diags * nv), bf16),
             pltpu.VMEM((2 * diags * nv, 2 * nv), bf16),
             pltpu.VMEM((sums, 8, nv), f32),
             pltpu.VMEM((sums, lanes), f32),
             pltpu.VMEM((sums, lanes), f32),
-            pltpu.SMEM(owner_times.shape, jnp.int32),
+            pltpu.SMEM(owner_times.shape[::-1], jnp.int32),
             pltpu.SMEM(diag_mom.shape, jnp.int32),
             pltpu.SMEM(diag_count.shape, jnp.int32),
             dma((4,)), dma((3,)), dma,
-            dma((2, n)), dma((n, 2)), dma((n, 2)), dma((n, 2)), dma((2,)), dma((2,)), dma((2,)),
+            dma((2, n, subs)), dma((n, 2, subs)), dma((n, 2, subs)), dma((n, 2, subs)),
+            dma((2, subs)), dma((2, subs)), dma((2,)),
         ],
         compiler_params=pltpu.CompilerParams(collective_id=0, has_side_effects=True),
         name="contract",
-    )(owner_times, diag_mom, diag_count, peram, src_elems)
-    return values.reshape(1, diags, 2, 2)
+    )(owner_times.T, diag_mom, diag_count, peram, src_elems)
+    return values
 
 
 def solution(mesh):

time: 109 us -> 110 us (level)
  Pallas kernels: 106 us -> 108 us
  local copies, waits for them, and re-layouts: 2.6 us -> 1.26 us
    pallas_call x1, Pallas kernels: 106 us -> 108 us  [shards(): pl.pallas_call(functools.partial(main_kernel, n, nspin, diags), out_shape...]
    reshape x1 -> x0, local copies, waits for them, and re-layouts: 1.26 us -> none  [shards(): return values.reshape(1, diags, 2, 2)]
where the time goes in v3:
time: 110 us
  Pallas kernels  108 us (98%)
  local copies, waits for them, and re-layouts  1.26 us (1%)
    pallas_call x1, Pallas kernels, shards(): pl.pallas_call(functools.partial(main_kernel, n, nspin, diags), out_shape...  108 us

profile of v3, /device:TPU:9, one launch (start us, length us, event | category | flops | bytes accessed | tf_op | source)
XLA Modules:
  0.0 109.9 jit_solution(12668820979411810148)
XLA Ops:
  0.7 108.0 %contract.1 = f32[1,2,2,2]{3,2,1,0:T(2,128)} custom-call(s32[2,8]{1,0:T(2,128)} %bitcast.1, s32[1,2,2]{2,1,0:T(2,128)} %mom_hbm.1, s32[1]{0:T(128)S(6)} %copy.7.count_hbm, bf16[128,24,2,512]{3,2,1,0:T(2,128)(2,1)} %peram_ref.1, bf16[7,2,256,256]{3,2,1,0:T(8,128)(2,1)} %elems_ref.1), custom_call_target="tpu_custom_call" | custom-call | tf_op jit(solution)/shard_map/contract/pallas_call | solution.py:365
  108.6 1.3 %copy.8 = f32[1,2,2,2]{3,2,1,0:T(2,128)} copy(f32[1,2,2,2]{3,2,1,0:T(2,128)} %contract.1) | data formatting | bytes 64

commit v4 on v3

--- a/solution.py
+++ b/solution.py
@@ -360,7 +360,7 @@
     any_spec = pl.BlockSpec(memory_space=pl.ANY)
     dma = pltpu.SemaphoreType.DMA
     sums = 6 * diags
-    subs = max(1, min(4, rows // 16 // 2))
+    subs = 1
     lanes = nv // 2
     values = pl.pallas_call(
         functools.partial(main_kernel, n, nspin, diags),

time: 110 us -> 109 us (level)
    pallas_call x1, Pallas kernels: 108 us -> 107 us  [shards(): pl.pallas_call(functools.partial(main_kernel, n, nspin, diags), out_shape...]
where the time goes in v4:
time: 109 us; the launch traced here: 108 us
  Pallas kernels  107 us (98%)
  local copies, waits for them, and re-layouts  1.26 us (1%)
    pallas_call x1, Pallas kernels, shards(): pl.pallas_call(functools.partial(main_kernel, n, nspin, diags), out_shape...  107 us

profile of v4, /device:TPU:9, one launch (start us, length us, event | category | flops | bytes accessed | tf_op | source)
XLA Modules:
  0.0 108.5 jit_solution(4861394645050190808)
XLA Ops:
  0.7 106.6 %contract.1 = f32[1,2,2,2]{3,2,1,0:T(2,128)} custom-call(s32[2,8]{1,0:T(2,128)} %bitcast.1, s32[1,2,2]{2,1,0:T(2,128)} %mom_hbm.1, s32[1]{0:T(128)S(6)} %copy.7.count_hbm, bf16[128,24,2,512]{3,2,1,0:T(2,128)(2,1)} %peram_ref.1, bf16[7,2,256,256]{3,2,1,0:T(8,128)(2,1)} %elems_ref.1), custom_call_target="tpu_custom_call" | custom-call | tf_op jit(solution)/shard_map/contract/pallas_call | solution.py:365
  107.2 1.3 %copy.8 = f32[1,2,2,2]{3,2,1,0:T(2,128)} copy(f32[1,2,2,2]{3,2,1,0:T(2,128)} %contract.1) | data formatting | bytes 64
